TPU v7x, 32 devices: a whole 2x2x4 slice. The times are simulated.
32 devices in a mesh: ax: 16 (over z, x, core), az: 2 (over y).
Axes of the slice: x: 2, y: 2, z: 4, core: 2. Of those that a mesh axis runs over, the one named last changes fastest.
Arguments:
- conserved: float32 [64, 5, 32, 512], P('ax', None, None, 'az'), may hold values from -1.1 to 6.2, as said below
- cycle_modes: int32 [32], replicated, may hold values from 1 to 64, as said below
- filtered_cycles: int32 [64], P('ax'), may hold values from 1 to 32, as said below
Outputs:
- stepped: float32 [64, 5, 32, 512], P('ax', None, None, 'az')
Inputs may be any that keep to these rules, and one draw needn't show every extreme that they name: `conserved`: density is at least 0.3 and pressure at least 0.02 in every cell. `cycle_modes`: 64 and 1 both occur. `filtered_cycles`: 32 and 1 both occur.
All inputs are finite; a program needn't handle non-finite values.
Results may differ from a plain program's by a relative error of at most 0.0003.
Values sent between devices are 32-bit elements; how exact they have to be, the bound alone decides.
No kernel may reach another device: no remote copies, remote signals or barrier semaphores. Data moves between devices by JAX's collectives and lax.ppermute only.
A program may use at most 64 MiB of HBM per device.

v0:
```python
import math
import jax
import jax.numpy as jnp
from jax import lax
from jax.sharding import PartitionSpec as P

NT = 512
NRF = 32
MODE_MOST = 64
STENCIL = (0.8, -0.2, 4.0 / 105.0, -1.0 / 280.0)
GAS_FACTOR = 0.4
TIME_STEP = 0.1


def extended(cells, sides, width, closed):
    for axis, dim in sides:
        count = lax.axis_size(axis)
        ends = count if closed else count - 1
        head = lax.slice_in_dim(cells, 0, width, axis=dim)
        tail = lax.slice_in_dim(cells, cells.shape[dim] - width, cells.shape[dim], axis=dim)
        cells = jnp.concatenate(
            [
                lax.ppermute(tail, axis, [(i, (i + 1) % count) for i in range(ends)]),
                cells,
                lax.ppermute(head, axis, [((i + 1) % count, i) for i in range(ends)]),
            ],
            axis=dim,
        )
    return cells


def partner(block, axis, distance):
    count = lax.axis_size(axis)
    route = []
    for low in range(count):
        high = low | 1 << distance
        if high != low and high < count:
            route += [(low, high), (high, low)]
    return lax.ppermute(block, axis, route)


def velocities(fields):
    density = fields[:, 0]
    axial_vel = fields[:, 1] / density
    radial_vel = fields[:, 2] / density
    swirl_vel = fields[:, 3] / density
    kinetic = fields[:, 1] * axial_vel + fields[:, 2] * radial_vel + fields[:, 3] * swirl_vel
    pressure = GAS_FACTOR * (fields[:, 4] - 0.5 * kinetic)
    return (axial_vel, radial_vel, swirl_vel, pressure)


def axial_flux(fields):
    axial_vel, radial_vel, swirl_vel, pressure = velocities(fields)
    return jnp.stack(
        [
            fields[:, 1],
            fields[:, 1] * axial_vel + pressure,
            fields[:, 2] * axial_vel,
            fields[:, 3] * axial_vel,
            axial_vel * (fields[:, 4] + pressure),
        ],
        axis=1,
    )


def radial_flux(fields):
    axial_vel, radial_vel, swirl_vel, pressure = velocities(fields)
    return jnp.stack(
        [
            fields[:, 2],
            fields[:, 1] * radial_vel,
            fields[:, 2] * radial_vel + pressure,
            fields[:, 3] * radial_vel,
            radial_vel * (fields[:, 4] + pressure),
        ],
        axis=1,
    )


def swirl_flux(fields):
    axial_vel, radial_vel, swirl_vel, pressure = velocities(fields)
    return jnp.stack(
        [
            fields[:, 3],
            fields[:, 1] * swirl_vel,
            fields[:, 2] * swirl_vel,
            fields[:, 3] * swirl_vel + pressure,
            swirl_vel * (fields[:, 4] + pressure),
        ],
        axis=1,
    )


def central_difference(values, along, extent):
    result = None
    for offset, weight in zip((1, 2, 3, 4), STENCIL):
        forward_part = lax.slice_in_dim(values, 4 + offset, 4 + offset + extent, axis=along)
        backward_part = lax.slice_in_dim(values, 4 - offset, 4 - offset + extent, axis=along)
        contribution = weight * (forward_part - backward_part)
        result = contribution if result is None else result + contribution
    return result


def section_update(axial_padded, theta_padded, opposite, fields):
    stations = fields.shape[0]
    radial = fields.shape[2]
    width = fields.shape[3]
    axial_term = central_difference(axial_flux(axial_padded), 0, stations)
    flips = jnp.array([1.0, 1.0, -1.0, -1.0, 1.0], jnp.float32).reshape(1, 5, 1, 1)
    mirrored = opposite[:, :, ::-1, :] * flips
    outer_rows = jnp.broadcast_to(fields[:, :, -1:, :], (stations, 5, 4, width))
    radial_padded = jnp.concatenate([mirrored, fields, outer_rows], axis=2)
    signed_radius = (jnp.arange(radial + 8, dtype=jnp.float32) - 3.5).reshape(1, 1, -1, 1)
    radial_term = central_difference(radial_flux(radial_padded) * signed_radius, 2, radial)
    swirl_term = central_difference(swirl_flux(theta_padded), 3, width) * (NT / (2.0 * math.pi))
    axial_vel, radial_vel, swirl_vel, pressure = velocities(fields)
    nothing = jnp.zeros_like(pressure)
    source = jnp.stack(
        [nothing, nothing, fields[:, 3] * swirl_vel + pressure, -fields[:, 2] * swirl_vel, nothing],
        axis=1,
    )
    radius = (jnp.arange(radial, dtype=jnp.float32) + 0.5).reshape(1, 1, -1, 1)
    tendency = -axial_term - (radial_term + swirl_term - source) / radius
    return fields + TIME_STEP * tendency


def fourier_basis(columns):
    harmonic = jnp.arange(2 * MODE_MOST, dtype=jnp.int32) % MODE_MOST
    product = columns[:, None] * harmonic[None, :] % NT
    angle = product.astype(jnp.float32) * (2.0 * math.pi / NT)
    cosine_side = (jnp.arange(2 * MODE_MOST, dtype=jnp.int32) < MODE_MOST)[None, :]
    return jnp.where(cosine_side, jnp.cos(angle), jnp.sin(angle))


def mode_weights(cycle_modes):
    harmonic = jnp.arange(2 * MODE_MOST, dtype=jnp.int32) % MODE_MOST
    base_weight = jnp.where(harmonic == 0, 1.0 / NT, 2.0 / NT).astype(jnp.float32)
    keep = harmonic[None, :] < cycle_modes[:, None]
    return jnp.where(keep, base_weight[None, :], 0.0)


def per_device(conserved, cycle_modes, filtered_cycles):
    axial_padded = extended(conserved, (("ax", 0),), 4, False)
    theta_padded = extended(conserved, (("az", 3),), 4, True)
    position = lax.axis_index("ax")
    last_index = lax.axis_size("ax") - 1
    low_edge = jnp.broadcast_to(conserved[:1], (4,) + conserved.shape[1:])
    high_edge = jnp.broadcast_to(conserved[-1:], (4,) + conserved.shape[1:])
    axial_padded = jnp.concatenate(
        [
            jnp.where(position == 0, low_edge, axial_padded[:4]),
            axial_padded[4:-4],
            jnp.where(position == last_index, high_edge, axial_padded[-4:]),
        ],
        axis=0,
    )
    partner_bit = lax.axis_size("az").bit_length() - 2
    opposite = partner(conserved[:, :, :4, :], "az", partner_bit)
    section = section_update(axial_padded, theta_padded, opposite, conserved)
    kept_weights = mode_weights(cycle_modes)
    sector = lax.axis_index("az")
    per_sector = NRF // lax.axis_size("az")
    lines = lax.all_to_all(section, "az", split_axis=2, concat_axis=3, tiled=True)
    full_basis = fourier_basis(jnp.arange(NT, dtype=jnp.int32))
    local_weights = lax.dynamic_slice_in_dim(kept_weights, sector * per_sector, per_sector, 0)
    coefficients = jnp.einsum("afrt,tc->afrc", lines, full_basis, precision=lax.Precision.HIGHEST)
    smoothed = jnp.einsum(
        "afrc,tc->afrt",
        coefficients * local_weights[None, None],
        full_basis,
        precision=lax.Precision.HIGHEST,
    )
    local_ids = sector * per_sector + jnp.arange(per_sector, dtype=jnp.int32)
    chosen = jnp.where(
        local_ids[None, None, :, None] < filtered_cycles[:, None, None, None], smoothed, lines
    )
    result_cycles = lax.all_to_all(chosen, "az", split_axis=3, concat_axis=2, tiled=True)
    return jnp.concatenate([result_cycles, section[:, :, NRF:, :]], axis=2)


def solution(mesh):
    placed = (P("ax", None, None, "az"), P(), P("ax"))
    return jax.shard_map(
        per_device, mesh=mesh, in_specs=placed, out_specs=P("ax", None, None, "az"), check_vma=False
    )
```

profile of v0, /device:TPU:0, one launch (start us, length us, event | category | flops | bytes accessed | tf_op | source)
XLA Modules:
  0.0 92.6 jit_solution(8275054431332127691)
XLA Ops:
  0.0 1.4 %collective-permute-start.1 = (f32[4,5,32,256]{3,2,1,0:T(8,128)}, f32[4,5,32,256]{3,2,1,0:T(8,128)S(1)}, u32[]{:S(2)}, u32[]{:S(2)}) collective-permute-start(f32[4,5,32,256]{3,2,1,0:T(8,128)} %param.4), channel_id=1, source_target_pairs={{2,0},{4,2},{6,4},{8,6},{10,8},{12,10},{14,12},{16,14},{18,16},{20... | collective-permute-start | bytes 1966088 | tf_op jit(solution)/shard_map/ppermute | solution.py:25
  1.4 3.1 %collective-permute-start = (f32[4,5,32,256]{3,2,1,0:T(8,128)}, f32[4,5,32,256]{3,2,1,0:T(8,128)S(1)}, u32[]{:S(2)}, u32[]{:S(2)}) collective-permute-start(f32[4,5,32,256]{3,2,1,0:T(8,128)} %param.4), channel_id=1, source_target_pairs={{0,2},{2,4},{4,6},{6,8},{8,10},{10,12},{12,14},{14,16},{16,18},{18... | collective-permute-start | bytes 1966088 | tf_op jit(solution)/shard_map/ppermute | solution.py:23
  4.5 1.2 %fusion.67 = (f32[4,5,32,4]{3,2,1,0:T(8,128)S(1)}, f32[4,5,32,4]{3,2,1,0:T(8,128)S(1)}) fusion(f32[4,5,32,256]{3,2,1,0:T(8,128)} %param.4), kind=kLoop, calls=%fused_computation.133 | loop fusion | bytes 40960 | tf_op jit(solution)/shard_map/slice | solution.py:20
  5.7 3.1 %collective-permute-start.3 = (f32[4,5,32,4]{3,2,1,0:T(8,128)S(1)}, f32[4,5,32,4]{3,2,1,0:T(8,128)S(1)}, u32[]{:S(2)}, u32[]{:S(2)}) collective-permute-start(f32[4,5,32,4]{3,2,1,0:T(8,128)S(1)} %get-tuple-element.18), channel_id=1, source_target_pairs={{0,1},{1,0},{2,3},{3,2},{4,5},{5,4},{6,7},{7,6},{8,9},{9,8},{10,11... | collective-permute-start | bytes 30728 | tf_op jit(solution)/shard_map/ppermute | solution.py:23
  8.8 0.1 collective-permute-start.4
  8.9 1.6 %slice.194 = f32[4,5,4,256]{3,2,1,0:T(4,128)} slice(f32[4,5,32,256]{3,2,1,0:T(8,128)} %param.4), slice={[0:4], [0:5], [0:4], [0:256]} | slice | bytes 163840 | tf_op jit(solution)/shard_map/slice | solution.py:158
  10.4 1.9 %collective-permute-start.2 = (f32[4,5,4,256]{3,2,1,0:T(4,128)}, f32[4,5,4,256]{3,2,1,0:T(4,128)}, u32[]{:S(2)}, u32[]{:S(2)}) collective-permute-start(f32[4,5,4,256]{3,2,1,0:T(4,128)} %slice.194), channel_id=1, source_target_pairs={{0,1},{1,0},{2,3},{3,2},{4,5},{5,4},{6,7},{7,6},{8,9},{9,8},{10,11... | collective-permute-start | bytes 245768 | tf_op jit(solution)/shard_map/ppermute | solution.py:39
  12.4 1.0 %slice_bitcast_fusion.1 = (f32[5,32,256]{2,1,0:T(8,128)S(1)}, f32[5,32,256]{2,1,0:T(8,128)S(1)}) fusion(f32[4,5,32,256]{3,2,1,0:T(8,128)} %param.4), kind=kLoop, calls=%fused_computation.103 | loop fusion | bytes 655360 | tf_op jit(solution)/shard_map/broadcast_in_dim | solution.py:147
  13.4 0.6 iota_add_fusion.1
  14.0 0.1 fusion.55
  14.1 0.5 and_select_fusion
  14.6 0.6 broadcast_compare_fusion
  15.2 0.6 compare_select_fusion.1
  15.8 0.6 slice.195
  16.4 0.7 copy.42
  17.1 0.6 copy.33
  17.8 0.1 pad.3.clone
  17.8 1.3 %dynamic-slice = s32[16]{0:T(128)} dynamic-slice(s32[32]{0:T(128)} %param.5, s32[]{:T(128)S(6)} %select_n.78), dynamic_slice_sizes={16} | dynamic-slice | bytes 132 | tf_op jit(solution)/shard_map/dynamic_slice | solution.py:165
  19.1 4.8 %collective-permute-done.4 = f32[4,5,32,4]{3,2,1,0:T(8,128)} collective-permute-done((f32[4,5,32,4]{3,2,1,0:T(8,128)S(1)}, f32[4,5,32,4]{3,2,1,0:T(8,128)}, u32[]{:S(2)}, u32[]{:S(2)}) %collective-permute-start.4) | collective-permute-done | bytes 10272 | tf_op jit(solution)/shard_map/ppermute | solution.py:25
  23.9 1.4 %pad_maximum_fusion.1 = f32[4,5,32,264]{3,2,1,0:T(8,128)S(1)} fusion(f32[4,5,32,4]{3,2,1,0:T(8,128)} %collective-permute-done.4, f32[4,5,32,256]{3,2,1,0:T(8,128)S(1)} %copy-done, f32[4,5,32,4]{3,2,1,0:T(8,128)S(1)} %collective-permute-done.3), kind=kLoop, calls=%fused_computation.3 | loop fusion | flops 337920 | bytes 1351680 | tf_op jit(solution)/shard_map/concatenate | solution.py:21
  25.4 0.1 add_dynamic-update-slice_fusion.1
  25.5 0.1 collective-permute-done.2
  25.7 1.5 %rev.3 = f32[4,5,4,256]{3,2,1,0:T(4,128)} reverse(f32[4,5,4,256]{3,2,1,0:T(4,128)} %collective-permute-done.2), dimensions={2} | reverse | bytes 163840 | tf_op jit(solution)/shard_map/rev | solution.py:110
  27.2 1.0 %broadcast_multiply_fusion.1 = f32[4,5,4,256]{3,2,1,0:T(4,128)S(1)} fusion(f32[4,5,4,256]{3,2,1,0:T(4,128)} %rev.3, f32[5]{0:T(128)S(1)} %copy-done.1), kind=kLoop, calls=%fused_computation.115 | loop fusion | flops 20480 | bytes 163860 | tf_op jit(solution)/shard_map/mul | solution.py:110
  28.1 0.8 broadcast_in_dim.74
  28.9 0.1 pad_maximum_fusion.2
  29.1 0.1 add_dynamic-update-slice_fusion.2
  29.3 0.4 copy-done.2
  29.7 0.1 broadcast_multiply_fusion
  30.0 0.2 pad_maximum_fusion
  30.3 0.2 add_dynamic-update-slice_fusion
  30.6 0.1 multiply_dynamic-update-slice_fusion
  30.7 1.5 %multiply_add_fusion = f32[4,5,32,256]{3,2,1,0:T(8,128)S(1)} fusion(f32[4,5,32,256]{3,2,1,0:T(8,128)S(1)} %copy-done, f32[4,1,32,256]{3,2,1,0:T(8,128)S(1)} %get-tuple-element.21, f32[4,1,32,256]{3,2,1,0:T(8,128)S(1)} %get-tuple-element.20, f32[4,5,32,264]{3,2,1,0:T(8,128)S(1)} %multiply_dynamic-update-slice_fusion.3, ...), kind=kLoop, calls=%fused_computation.45 | loop fusion | flops 7208960 | bytes 17301672 | tf_op jit(solution)/shard_map/add | solution.py:124
  32.3 1.4 %copy.34 = f32[4,5,32,256]{3,1,0,2:T(8,128)} copy(f32[4,5,32,256]{3,2,1,0:T(8,128)S(1)} %multiply_add_fusion) | data formatting | bytes 1310720 | tf_op jit(solution)/shard_map/add | solution.py:124
  33.7 3.7 %all-to-all-start = ((f32[4,5,32,256]{3,1,0,2:T(8,128)}), f32[4,5,32,256]{3,1,0,2:T(8,128)S(1)}, u32[]{:S(2)}, u32[]{:S(2)}) async-start(f32[4,5,32,256]{3,1,0,2:T(8,128)} %copy.34), calls=%async_computation | async-start | bytes 2097152 | tf_op jit(solution)/shard_map/all_to_all | solution.py:163
  37.5 0.1 compare_select_fusion
  37.5 15.0 %all-to-all-done = f32[4,5,32,256]{3,1,0,2:T(8,128)S(1)} async-done(((f32[4,5,32,256]{3,1,0,2:T(8,128)}), f32[4,5,32,256]{3,1,0,2:T(8,128)S(1)}, u32[]{:S(2)}, u32[]{:S(2)}) %all-to-all-start) | async-done | bytes 655392 | tf_op jit(solution)/shard_map/all_to_all | solution.py:163
  52.5 0.5 copy.41
  53.0 0.5 all_to_all.29
  53.5 1.7 %convolution_multiply_fusion = f32[4,5,16,128]{3,2,1,0:T(8,128)S(1)} fusion(f32[4,5,16,512]{3,2,1,0:T(8,128)S(1)} %all_to_all.29, s32[128]{0:T(128)S(1)} %copy-done.3, pred[128]{0:T(512)(128)(4,1)S(1)} %iota_compare_fusion, f32[16,128]{1,0:T(8,128)S(1)} %compare_select_fusion), kind=kOutput, calls=%fused_computation.2 | convolution fusion | flops 252682240 | bytes 828032 | tf_op jit(solution)/shard_map/afrt,tc->afrc/dot_general | solution.py:166
  55.3 1.7 %convolution_select_fusion = f32[4,5,16,512]{3,2,1,0:T(8,128)S(1)} fusion(f32[4,5,16,512]{3,2,1,0:T(8,128)S(1)} %all_to_all.29, f32[4,5,16,128]{3,2,1,0:T(8,128)S(1)} %convolution_multiply_fusion, pred[4,16]{1,0:T(4,128)(4,1)S(1)} %copy-done.7, s32[128]{0:T(128)S(1)} %copy-done.3, pred[128]{0:T(512)(128)(4,1)S(1)} %iota_compare_fusion), kind=kOutput, calls=%fused_computation.1 | convolution fusion | flops 252805120 | bytes 1475264 | tf_op jit(solution)/shard_map/afrc,tc->afrt/dot_general | solution.py:167
  57.0 3.5 %copy.36 = f32[4,5,16,512]{2,0,1,3:T(4,128)} copy(f32[4,5,16,512]{3,2,1,0:T(8,128)S(1)} %convolution_select_fusion) | data formatting | bytes 1310720 | tf_op jit(solution)/shard_map/jit(_where)/select_n | solution.py:174
  60.5 5.7 %reshape.69 = f32[2,1,81920]{2,1,0:T(1,128)S(1)} reshape(f32[512,5,4,16]{3,2,1,0:T(4,128)} %bitcast.27) | data formatting | bytes 1310720
  66.2 12.1 %all_to_all.36 = f32[2,1,81920]{2,1,0:T(1,128)S(1)} all-to-all(f32[2,1,81920]{2,1,0:T(1,128)S(1)} %reshape.69), channel_id=1, replica_groups=mesh['ax'=16,'az'=2] {'az'}, dimensions={0} | all-to-all | bytes 1310720 | tf_op jit(solution)/shard_map/all_to_all | solution.py:177
  78.3 0.5 broadcast.144
  78.8 2.7 %reduce = f32[2,81920]{1,0:T(2,128)S(1)} reduce(f32[2,1,81920]{2,1,0:T(1,128)S(1)} %all_to_all.36, f32[]{:T(128)} %broadcast.144), dimensions={1}, to_apply=%all_to_all.30.reduce_sub_computation | reduce | bytes 1310724 | tf_op jit(solution)/shard_map/all_to_all | solution.py:177
  81.5 6.3 %reshape.70 = f32[512,5,4,16]{3,2,1,0:T(4,128)} reshape(f32[2,81920]{1,0:T(2,128)S(1)} %reduce) | data formatting | bytes 1310720
  87.8 4.8 %copy.37 = f32[4,5,2,16,256]{4,3,2,1,0:T(8,128)} copy(f32[4,5,2,16,256]{3,0,1,4,2:T(4,128)} %bitcast.28) | data formatting | bytes 1310720 | tf_op jit(solution)/shard_map/all_to_all | solution.py:177
  (36 shorter events, 0.6 us)
Async XLA Ops:
  0.0 14.0 %copy-start = (f32[4,5,32,256]{3,2,1,0:T(8,128)S(1)}, f32[4,5,32,256]{3,2,1,0:T(8,128)}, u32[]{:S(2)}) copy-start(f32[4,5,32,256]{3,2,1,0:T(8,128)} %param.4) | copy-start | bytes 1966084
  0.0 14.6 %copy-start.6 = (s32[4]{0:T(128)S(1)}, s32[4]{0:T(128)}, u32[]{:S(2)}) copy-start(s32[4]{0:T(128)} %param.6) | copy-start | bytes 52
  0.0 29.8 %collective-permute-start.1 = (f32[4,5,32,256]{3,2,1,0:T(8,128)}, f32[4,5,32,256]{3,2,1,0:T(8,128)S(1)}, u32[]{:S(2)}, u32[]{:S(2)}) collective-permute-start(f32[4,5,32,256]{3,2,1,0:T(8,128)} %param.4), channel_id=1, source_target_pairs={{2,0},{4,2},{6,4},{8,6},{10,8},{12,10},{14,12},{16,14},{18,16},{20... | collective-permute-start | bytes 1966088 | tf_op jit(solution)/shard_map/ppermute | solution.py:25
  1.4 28.5 %collective-permute-start = (f32[4,5,32,256]{3,2,1,0:T(8,128)}, f32[4,5,32,256]{3,2,1,0:T(8,128)S(1)}, u32[]{:S(2)}, u32[]{:S(2)}) collective-permute-start(f32[4,5,32,256]{3,2,1,0:T(8,128)} %param.4), channel_id=1, source_target_pairs={{0,2},{2,4},{4,6},{6,8},{8,10},{10,12},{12,14},{14,16},{16,18},{18... | collective-permute-start | bytes 1966088 | tf_op jit(solution)/shard_map/ppermute | solution.py:23
  5.7 13.4 %collective-permute-start.3 = (f32[4,5,32,4]{3,2,1,0:T(8,128)S(1)}, f32[4,5,32,4]{3,2,1,0:T(8,128)S(1)}, u32[]{:S(2)}, u32[]{:S(2)}) collective-permute-start(f32[4,5,32,4]{3,2,1,0:T(8,128)S(1)} %get-tuple-element.18), channel_id=1, source_target_pairs={{0,1},{1,0},{2,3},{3,2},{4,5},{5,4},{6,7},{7,6},{8,9},{9,8},{10,11... | collective-permute-start | bytes 30728 | tf_op jit(solution)/shard_map/ppermute | solution.py:23
  8.8 15.1 %collective-permute-start.4 = (f32[4,5,32,4]{3,2,1,0:T(8,128)S(1)}, f32[4,5,32,4]{3,2,1,0:T(8,128)}, u32[]{:S(2)}, u32[]{:S(2)}) collective-permute-start(f32[4,5,32,4]{3,2,1,0:T(8,128)S(1)} %get-tuple-element.19), channel_id=1, source_target_pairs={{1,0},{0,1},{3,2},{2,3},{5,4},{4,5},{7,6},{6,7},{9,8},{8,9},{11,10... | collective-permute-start | bytes 30728 | tf_op jit(solution)/shard_map/ppermute | solution.py:25
  10.4 15.2 %collective-permute-start.2 = (f32[4,5,4,256]{3,2,1,0:T(4,128)}, f32[4,5,4,256]{3,2,1,0:T(4,128)}, u32[]{:S(2)}, u32[]{:S(2)}) collective-permute-start(f32[4,5,4,256]{3,2,1,0:T(4,128)} %slice.194), channel_id=1, source_target_pairs={{0,1},{1,0},{2,3},{3,2},{4,5},{5,4},{6,7},{7,6},{8,9},{9,8},{10,11... | collective-permute-start | bytes 245768 | tf_op jit(solution)/shard_map/ppermute | solution.py:39
  25.3 1.9 %copy-start.1 = (f32[5]{0:T(128)S(1)}, f32[5]{0:T(128)}, u32[]{:S(2)}) copy-start(f32[5]{0:T(128)} %constant.88.clone) | copy-start | bytes 64
  29.0 0.7 copy-start.2
  32.3 5.2 %copy-start.3 = (s32[128]{0:T(128)S(1)}, s32[128]{0:T(128)}, u32[]{:S(2)}) copy-start(s32[128]{0:T(128)} %and_select_fusion) | copy-start | bytes 1540
  32.3 5.2 %copy-start.4 = (f32[128]{0:T(128)S(1)}, f32[128]{0:T(128)}, u32[]{:S(2)}) copy-start(f32[128]{0:T(128)} %compare_select_fusion.1) | copy-start | bytes 1540
  32.3 5.2 %copy-start.5 = (s32[16]{0:T(128)S(1)}, s32[16]{0:T(128)}, u32[]{:S(2)}) copy-start(s32[16]{0:T(128)} %dynamic-slice) | copy-start | bytes 196
  33.7 18.8 %all-to-all-start = ((f32[4,5,32,256]{3,1,0,2:T(8,128)}), f32[4,5,32,256]{3,1,0,2:T(8,128)S(1)}, u32[]{:S(2)}, u32[]{:S(2)}) async-start(f32[4,5,32,256]{3,1,0,2:T(8,128)} %copy.34), calls=%async_computation | async-start | bytes 2097152 | tf_op jit(solution)/shard_map/all_to_all | solution.py:163
  52.5 2.8 %copy-start.7 = (pred[4,16]{1,0:T(4,128)(4,1)S(1)}, pred[4,16]{1,0:T(4,128)(4,1)}, u32[]{:S(2)}) copy-start(pred[4,16]{1,0:T(4,128)(4,1)} %broadcast_compare_fusion) | copy-start | bytes 196
where the time goes:
time: 93.3 us; the launch traced here: 92.6 us
  local copies, waits for them, and re-layouts  33.1 us (35%)
  waiting for transfers between devices  19.9 us (21%)
  starting transfers between devices  13.3 us (14%)
  blocking collectives  12.1 us (13%)
  other arithmetic  10.5 us (11%)
  matrix products  3.43 us (4%)
    all_to_all x1, waiting for transfers between devices, per_device(): lax.all_to_all(section, 'az', split_axis=2, concat_axis=3, tiled=True)  15 us
    unnamed x21, local copies, waits for them, and re-layouts  12.5 us
    all_to_all x1, blocking collectives, per_device(): lax.all_to_all(chosen, 'az', split_axis=3, concat_axis=2, tiled=True)  12.1 us
    ppermute x2, starting transfers between devices, extended(): lax.ppermute(tail, axis, [(i, (i + 1) % count) for i in range(ends)])  6.14 us
    all_to_all x2, local copies, waits for them, and re-layouts, per_device(): lax.all_to_all(chosen, 'az', split_axis=3, concat_axis=2, tiled=True)  5.32 us
    ppermute x2, waiting for transfers between devices, extended(): lax.ppermute(head, axis, [((i + 1) % count, i) for i in range(ends)])  4.79 us
    all_to_all x1, starting transfers between devices, per_device(): lax.all_to_all(section, 'az', split_axis=2, concat_axis=3, tiled=True)  3.75 us
    select_n x1, local copies, waits for them, and re-layouts, per_device(): jnp.where(local_ids[None, None, :, None] < filtered_cycles[:, None, None,...  3.52 us
  transfers between devices with their start and end apart: 6, of which 3 were waited for; matrix products, arithmetic and copies ran while one was open for 16% of the time, Pallas kernels for 0%

commit v1 on v0

--- a/solution.py
+++ b/solution.py
@@ -174,7 +174,9 @@
     chosen = jnp.where(
         local_ids[None, None, :, None] < filtered_cycles[:, None, None, None], smoothed, lines
     )
-    result_cycles = lax.all_to_all(chosen, "az", split_axis=3, concat_axis=2, tiled=True)
+    parts = jnp.split(chosen, lax.axis_size("az"), axis=3)
+    incoming = lax.all_to_all(jnp.stack(parts), "az", 0, 0)
+    result_cycles = jnp.concatenate(incoming, axis=2)
     return jnp.concatenate([result_cycles, section[:, :, NRF:, :]], axis=2)
 
 

time: 93.3 us -> 70.7 us (0.76)
  local copies, waits for them, and re-layouts: 33.1 us -> 12.6 us
  other arithmetic: 10.5 us -> 7.8 us
    unnamed x21, local copies, waits for them, and re-layouts: 12.5 us -> 0.48 us
    all_to_all x2 -> x0, local copies, waits for them, and re-layouts: 5.32 us -> none  [per_device(): lax.all_to_all(chosen, 'az', split_axis=3, concat_axis=2, tiled=True)]
    select_n x1 -> x0, local copies, waits for them, and re-layouts: 3.52 us -> none  [per_device(): jnp.where(local_ids[None, None, :, None] < filtered_cycles[:, None, None,...]
    all_to_all x1 -> x0, other arithmetic: 2.7 us -> none  [per_device(): lax.all_to_all(chosen, 'az', split_axis=3, concat_axis=2, tiled=True)]
  transfers between devices with their start and end apart: 6 -> 6, of which waited for: 3 -> 3; matrix products, arithmetic and copies ran while one was open for 16% -> 20% of each run, Pallas kernels for 0% -> 0%
where the time goes in v1:
time: 70.7 us; the launch traced here: 70.1 us
  waiting for transfers between devices  20.5 us (29%)
  starting transfers between devices  13.3 us (19%)
  local copies, waits for them, and re-layouts  12.6 us (18%)
  blocking collectives  12.1 us (17%)
  other arithmetic  7.8 us (11%)
  matrix products  3.43 us (5%)
    all_to_all x1, waiting for transfers between devices, per_device(): lax.all_to_all(section, 'az', split_axis=2, concat_axis=3, tiled=True)  15 us
    all_to_all x1, blocking collectives, per_device(): incoming = lax.all_to_all(jnp.stack(parts), 'az', 0, 0)  12.1 us
    ppermute x2, starting transfers between devices, extended(): lax.ppermute(tail, axis, [(i, (i + 1) % count) for i in range(ends)])  6.15 us
    ppermute x2, waiting for transfers between devices, extended(): lax.ppermute(head, axis, [((i + 1) % count, i) for i in range(ends)])  5.4 us
    all_to_all x1, starting transfers between devices, per_device(): lax.all_to_all(section, 'az', split_axis=2, concat_axis=3, tiled=True)  3.75 us
    ppermute x1, starting transfers between devices, partner(): return lax.ppermute(block, axis, route)  1.95 us
    dot_general x1, matrix products, per_device(): jnp.einsum('afrt,tc->afrc', lines, full_basis, precision=lax.Precision.HI...  1.72 us
    dot_general x1, matrix products, per_device(): jnp.einsum('afrc,tc->afrt', coefficients * local_weights[None, None], ful...  1.72 us
  transfers between devices with their start and end apart: 6, of which 3 were waited for; matrix products, arithmetic and copies ran while one was open for 20% of the time, Pallas kernels for 0%

profile of v1, /device:TPU:0, one launch (start us, length us, event | category | flops | bytes accessed | tf_op | source)
XLA Modules:
  0.0 70.1 jit_solution(7643926990583324465)
XLA Ops:
  0.0 1.4 %collective-permute-start.1 = (f32[4,5,32,256]{3,2,1,0:T(8,128)}, f32[4,5,32,256]{3,2,1,0:T(8,128)S(1)}, u32[]{:S(2)}, u32[]{:S(2)}) collective-permute-start(f32[4,5,32,256]{3,2,1,0:T(8,128)} %param.4), channel_id=1, source_target_pairs={{2,0},{4,2},{6,4},{8,6},{10,8},{12,10},{14,12},{16,14},{18,16},{20... | collective-permute-start | bytes 1966088 | tf_op jit(solution)/shard_map/ppermute | solution.py:25
  1.4 3.1 %collective-permute-start = (f32[4,5,32,256]{3,2,1,0:T(8,128)}, f32[4,5,32,256]{3,2,1,0:T(8,128)S(1)}, u32[]{:S(2)}, u32[]{:S(2)}) collective-permute-start(f32[4,5,32,256]{3,2,1,0:T(8,128)} %param.4), channel_id=1, source_target_pairs={{0,2},{2,4},{4,6},{6,8},{8,10},{10,12},{12,14},{14,16},{16,18},{18... | collective-permute-start | bytes 1966088 | tf_op jit(solution)/shard_map/ppermute | solution.py:23
  4.5 1.2 %fusion.67 = (f32[4,5,32,4]{3,2,1,0:T(8,128)S(1)}, f32[4,5,32,4]{3,2,1,0:T(8,128)S(1)}) fusion(f32[4,5,32,256]{3,2,1,0:T(8,128)} %param.4), kind=kLoop, calls=%fused_computation.136 | loop fusion | bytes 40960 | tf_op jit(solution)/shard_map/slice | solution.py:20
  5.7 3.1 %collective-permute-start.3 = (f32[4,5,32,4]{3,2,1,0:T(8,128)S(1)}, f32[4,5,32,4]{3,2,1,0:T(8,128)S(1)}, u32[]{:S(2)}, u32[]{:S(2)}) collective-permute-start(f32[4,5,32,4]{3,2,1,0:T(8,128)S(1)} %get-tuple-element.20), channel_id=1, source_target_pairs={{0,1},{1,0},{2,3},{3,2},{4,5},{5,4},{6,7},{7,6},{8,9},{9,8},{10,11... | collective-permute-start | bytes 30728 | tf_op jit(solution)/shard_map/ppermute | solution.py:23
  8.8 0.1 collective-permute-start.4
  8.9 1.6 %slice.194 = f32[4,5,4,256]{3,2,1,0:T(4,128)} slice(f32[4,5,32,256]{3,2,1,0:T(8,128)} %param.4), slice={[0:4], [0:5], [0:4], [0:256]} | slice | bytes 163840 | tf_op jit(solution)/shard_map/slice | solution.py:158
  10.5 1.9 %collective-permute-start.2 = (f32[4,5,4,256]{3,2,1,0:T(4,128)}, f32[4,5,4,256]{3,2,1,0:T(4,128)}, u32[]{:S(2)}, u32[]{:S(2)}) collective-permute-start(f32[4,5,4,256]{3,2,1,0:T(4,128)} %slice.194), channel_id=1, source_target_pairs={{0,1},{1,0},{2,3},{3,2},{4,5},{5,4},{6,7},{7,6},{8,9},{9,8},{10,11... | collective-permute-start | bytes 245768 | tf_op jit(solution)/shard_map/ppermute | solution.py:39
  12.4 1.0 %slice_bitcast_fusion.3 = (f32[5,32,256]{2,1,0:T(8,128)S(1)}, f32[5,32,256]{2,1,0:T(8,128)S(1)}) fusion(f32[4,5,32,256]{3,2,1,0:T(8,128)} %param.4), kind=kLoop, calls=%fused_computation.106 | loop fusion | bytes 655360 | tf_op jit(solution)/shard_map/broadcast_in_dim | solution.py:147
  13.4 0.5 iota_add_fusion.1
  14.0 0.1 fusion.55
  14.1 0.5 and_select_fusion
  14.6 0.6 broadcast_compare_fusion
  15.2 0.6 compare_select_fusion.1
  15.8 0.6 slice.195
  16.4 0.7 %copy.39 = f32[4,5,1,256]{3,0,1,2:T(4,128)S(1)} copy(f32[4,5,1,256]{3,2,1,0:T(1,128)} %slice.195) | data formatting | bytes 40960 | tf_op jit(solution)/shard_map/slice | solution.py:111
  17.2 0.6 copy.31
  17.8 0.1 pad.5.clone
  17.9 0.6 dynamic-slice
  18.5 5.4 %collective-permute-done.4 = f32[4,5,32,4]{3,2,1,0:T(8,128)} collective-permute-done((f32[4,5,32,4]{3,2,1,0:T(8,128)S(1)}, f32[4,5,32,4]{3,2,1,0:T(8,128)}, u32[]{:S(2)}, u32[]{:S(2)}) %collective-permute-start.4) | collective-permute-done | bytes 10272 | tf_op jit(solution)/shard_map/ppermute | solution.py:25
  23.9 1.4 %pad_maximum_fusion.1 = f32[4,5,32,264]{3,2,1,0:T(8,128)S(1)} fusion(f32[4,5,32,4]{3,2,1,0:T(8,128)} %collective-permute-done.4, f32[4,5,32,256]{3,2,1,0:T(8,128)S(1)} %copy-done, f32[4,5,32,4]{3,2,1,0:T(8,128)S(1)} %collective-permute-done.3), kind=kLoop, calls=%fused_computation.3 | loop fusion | flops 337920 | bytes 1351680 | tf_op jit(solution)/shard_map/concatenate | solution.py:21
  25.4 0.1 add_dynamic-update-slice_fusion.1
  25.5 0.1 collective-permute-done.2
  25.7 1.5 %rev.3 = f32[4,5,4,256]{3,2,1,0:T(4,128)} reverse(f32[4,5,4,256]{3,2,1,0:T(4,128)} %collective-permute-done.2), dimensions={2} | reverse | bytes 163840 | tf_op jit(solution)/shard_map/rev | solution.py:110
  27.2 1.0 %broadcast_multiply_fusion.1 = f32[4,5,4,256]{3,2,1,0:T(4,128)S(1)} fusion(f32[4,5,4,256]{3,2,1,0:T(4,128)} %rev.3, f32[5]{0:T(128)S(1)} %copy-done.1), kind=kLoop, calls=%fused_computation.118 | loop fusion | flops 20480 | bytes 163860 | tf_op jit(solution)/shard_map/mul | solution.py:110
  28.2 0.8 %broadcast_in_dim.74 = f32[4,5,4,256]{3,2,1,0:T(4,128)S(1)} broadcast(f32[4,5,256]{2,1,0:T(8,128)} %copy.31), dimensions={0,1,3} | broadcast | bytes 102400 | tf_op jit(solution)/shard_map/broadcast_in_dim | solution.py:111
  28.9 0.1 pad_maximum_fusion.2
  29.1 0.1 add_dynamic-update-slice_fusion.2
  29.3 0.4 copy-done.2
  29.7 0.1 broadcast_multiply_fusion
  29.8 0.1 broadcast_select_fusion
  29.9 0.1 broadcast_select_fusion.1
  30.0 0.2 pad_maximum_fusion
  30.2 0.2 add_dynamic-update-slice_fusion
  30.4 0.1 multiply_dynamic-update-slice_fusion.2
  30.5 0.1 multiply_dynamic-update-slice_fusion.1
  30.6 0.1 multiply_dynamic-update-slice_fusion
  30.7 1.5 %multiply_add_fusion = f32[4,5,32,256]{3,2,1,0:T(8,128)S(1)} fusion(f32[4,5,32,256]{3,2,1,0:T(8,128)S(1)} %copy-done, f32[4,1,32,256]{3,2,1,0:T(8,128)S(1)} %get-tuple-element.23, f32[4,1,32,256]{3,2,1,0:T(8,128)S(1)} %get-tuple-element.22, f32[4,5,32,264]{3,2,1,0:T(8,128)S(1)} %multiply_dynamic-update-slice_fusion.3, ...), kind=kLoop, calls=%fused_computation.46 | loop fusion | flops 7208960 | bytes 17301672 | tf_op jit(solution)/shard_map/add | solution.py:124
  32.2 1.4 %copy.32 = f32[4,5,32,256]{3,1,0,2:T(8,128)} copy(f32[4,5,32,256]{3,2,1,0:T(8,128)S(1)} %multiply_add_fusion) | data formatting | bytes 1310720 | tf_op jit(solution)/shard_map/add | solution.py:124
  33.6 3.7 %all-to-all-start = ((f32[4,5,32,256]{3,1,0,2:T(8,128)}), f32[4,5,32,256]{3,1,0,2:T(8,128)S(1)}, u32[]{:S(2)}, u32[]{:S(2)}) async-start(f32[4,5,32,256]{3,1,0,2:T(8,128)} %copy.32), calls=%async_computation | async-start | bytes 2097152 | tf_op jit(solution)/shard_map/all_to_all | solution.py:163
  37.4 0.1 compare_select_fusion
  37.5 15.0 %all-to-all-done = f32[4,5,32,256]{3,1,0,2:T(8,128)S(1)} async-done(((f32[4,5,32,256]{3,1,0,2:T(8,128)}), f32[4,5,32,256]{3,1,0,2:T(8,128)S(1)}, u32[]{:S(2)}, u32[]{:S(2)}) %all-to-all-start) | async-done | bytes 655392 | tf_op jit(solution)/shard_map/all_to_all | solution.py:163
  52.4 0.5 copy.38
  53.0 0.5 all_to_all.19
  53.5 1.7 %convolution_multiply_fusion = f32[4,5,16,128]{3,2,1,0:T(8,128)S(1)} fusion(f32[4,5,16,512]{3,2,1,0:T(8,128)S(1)} %all_to_all.19, s32[128]{0:T(128)S(1)} %copy-done.3, pred[128]{0:T(512)(128)(4,1)S(1)} %iota_compare_fusion, f32[16,128]{1,0:T(8,128)S(1)} %compare_select_fusion), kind=kOutput, calls=%fused_computation.2 | convolution fusion | flops 252682240 | bytes 828032 | tf_op jit(solution)/shard_map/afrt,tc->afrc/dot_general | solution.py:166
  55.2 1.7 %convolution_select_fusion = f32[4,5,16,512]{3,2,1,0:T(8,128)S(1)} fusion(f32[4,5,16,512]{3,2,1,0:T(8,128)S(1)} %all_to_all.19, f32[4,5,16,128]{3,2,1,0:T(8,128)S(1)} %convolution_multiply_fusion, pred[4,16]{1,0:T(4,128)(4,1)S(1)} %copy-done.8, s32[128]{0:T(128)S(1)} %copy-done.3, pred[128]{0:T(512)(128)(4,1)S(1)} %iota_compare_fusion), kind=kOutput, calls=%fused_computation.1 | convolution fusion | flops 252805120 | bytes 1475264 | tf_op jit(solution)/shard_map/afrc,tc->afrt/dot_general | solution.py:167
  56.9 0.1 slice_bitcast_fusion.1
  57.1 12.1 %all_to_all.23 = f32[2,4,5,16,256]{4,3,2,1,0:T(8,128)S(1)} all-to-all(f32[2,4,5,16,256]{4,3,2,1,0:T(8,128)S(1)} %pad_maximum_fusion.3), channel_id=1, replica_groups=mesh['ax'=16,'az'=2] {'az'}, dimensions={0} | all-to-all | bytes 1310720 | tf_op jit(solution)/shard_map/all_to_all | solution.py:178
  69.2 0.9 %copy.34 = f32[4,5,2,16,256]{4,3,2,1,0:T(8,128)} copy(f32[4,5,2,16,256]{4,3,1,0,2:T(8,128)S(1)} %bitcast.29) | data formatting | bytes 1310720 | tf_op jit(solution)/shard_map/reshape | solution.py:179
  (35 shorter events, 0.4 us)
Async XLA Ops:
  0.0 14.0 %copy-start = (f32[4,5,32,256]{3,2,1,0:T(8,128)S(1)}, f32[4,5,32,256]{3,2,1,0:T(8,128)}, u32[]{:S(2)}) copy-start(f32[4,5,32,256]{3,2,1,0:T(8,128)} %param.4) | copy-start | bytes 1966084
  0.0 14.6 %copy-start.6 = (s32[4]{0:T(128)S(1)}, s32[4]{0:T(128)}, u32[]{:S(2)}) copy-start(s32[4]{0:T(128)} %param.6) | copy-start | bytes 52
  0.0 17.8 %copy-start.7 = (s32[32]{0:T(128)S(1)}, s32[32]{0:T(128)}, u32[]{:S(2)}) copy-start(s32[32]{0:T(128)} %param.5) | copy-start | bytes 388
  0.0 29.8 %collective-permute-start.1 = (f32[4,5,32,256]{3,2,1,0:T(8,128)}, f32[4,5,32,256]{3,2,1,0:T(8,128)S(1)}, u32[]{:S(2)}, u32[]{:S(2)}) collective-permute-start(f32[4,5,32,256]{3,2,1,0:T(8,128)} %param.4), channel_id=1, source_target_pairs={{2,0},{4,2},{6,4},{8,6},{10,8},{12,10},{14,12},{16,14},{18,16},{20... | collective-permute-start | bytes 1966088 | tf_op jit(solution)/shard_map/ppermute | solution.py:25
  1.4 28.5 %collective-permute-start = (f32[4,5,32,256]{3,2,1,0:T(8,128)}, f32[4,5,32,256]{3,2,1,0:T(8,128)S(1)}, u32[]{:S(2)}, u32[]{:S(2)}) collective-permute-start(f32[4,5,32,256]{3,2,1,0:T(8,128)} %param.4), channel_id=1, source_target_pairs={{0,2},{2,4},{4,6},{6,8},{8,10},{10,12},{12,14},{14,16},{16,18},{18... | collective-permute-start | bytes 1966088 | tf_op jit(solution)/shard_map/ppermute | solution.py:23
  5.7 12.8 %collective-permute-start.3 = (f32[4,5,32,4]{3,2,1,0:T(8,128)S(1)}, f32[4,5,32,4]{3,2,1,0:T(8,128)S(1)}, u32[]{:S(2)}, u32[]{:S(2)}) collective-permute-start(f32[4,5,32,4]{3,2,1,0:T(8,128)S(1)} %get-tuple-element.20), channel_id=1, source_target_pairs={{0,1},{1,0},{2,3},{3,2},{4,5},{5,4},{6,7},{7,6},{8,9},{9,8},{10,11... | collective-permute-start | bytes 30728 | tf_op jit(solution)/shard_map/ppermute | solution.py:23
  8.8 15.1 %collective-permute-start.4 = (f32[4,5,32,4]{3,2,1,0:T(8,128)S(1)}, f32[4,5,32,4]{3,2,1,0:T(8,128)}, u32[]{:S(2)}, u32[]{:S(2)}) collective-permute-start(f32[4,5,32,4]{3,2,1,0:T(8,128)S(1)} %get-tuple-element.21), channel_id=1, source_target_pairs={{1,0},{0,1},{3,2},{2,3},{5,4},{4,5},{7,6},{6,7},{9,8},{8,9},{11,10... | collective-permute-start | bytes 30728 | tf_op jit(solution)/shard_map/ppermute | solution.py:25
  10.5 15.2 %collective-permute-start.2 = (f32[4,5,4,256]{3,2,1,0:T(4,128)}, f32[4,5,4,256]{3,2,1,0:T(4,128)}, u32[]{:S(2)}, u32[]{:S(2)}) collective-permute-start(f32[4,5,4,256]{3,2,1,0:T(4,128)} %slice.194), channel_id=1, source_target_pairs={{0,1},{1,0},{2,3},{3,2},{4,5},{5,4},{6,7},{7,6},{8,9},{9,8},{10,11... | collective-permute-start | bytes 245768 | tf_op jit(solution)/shard_map/ppermute | solution.py:39
  25.3 1.9 %copy-start.1 = (f32[5]{0:T(128)S(1)}, f32[5]{0:T(128)}, u32[]{:S(2)}) copy-start(f32[5]{0:T(128)} %constant.88.clone) | copy-start | bytes 64
  29.0 0.6 copy-start.2
  32.2 5.2 %copy-start.3 = (s32[128]{0:T(128)S(1)}, s32[128]{0:T(128)}, u32[]{:S(2)}) copy-start(s32[128]{0:T(128)} %and_select_fusion) | copy-start | bytes 1540
  32.2 5.2 %copy-start.4 = (f32[128]{0:T(128)S(1)}, f32[128]{0:T(128)}, u32[]{:S(2)}) copy-start(f32[128]{0:T(128)} %compare_select_fusion.1) | copy-start | bytes 1540
  32.2 5.2 %copy-start.5 = (s32[16]{0:T(128)S(1)}, s32[16]{0:T(128)}, u32[]{:S(2)}) copy-start(s32[16]{0:T(128)} %dynamic-slice) | copy-start | bytes 196
  33.6 18.8 %all-to-all-start = ((f32[4,5,32,256]{3,1,0,2:T(8,128)}), f32[4,5,32,256]{3,1,0,2:T(8,128)S(1)}, u32[]{:S(2)}, u32[]{:S(2)}) async-start(f32[4,5,32,256]{3,1,0,2:T(8,128)} %copy.32), calls=%async_computation | async-start | bytes 2097152 | tf_op jit(solution)/shard_map/all_to_all | solution.py:163
  52.4 2.8 %copy-start.8 = (pred[4,16]{1,0:T(4,128)(4,1)S(1)}, pred[4,16]{1,0:T(4,128)(4,1)}, u32[]{:S(2)}) copy-start(pred[4,16]{1,0:T(4,128)(4,1)} %broadcast_compare_fusion) | copy-start | bytes 196
